TPU v7x, 32 devices: a whole 2x2x4 slice. The times are simulated.
32 devices in a mesh: dp: 2 (over y), head: 16 (over z, x, core).
Axes of the slice: x: 2, y: 2, z: 4, core: 2. Of those that a mesh axis runs over, the one named last changes fastest.
Arguments:
- head_ids: int32 [2, 2048, 8], P('dp', 'head'), may hold values from 0 to 63, as said below
- query_slots: bfloat16 [2, 2048, 8, 128], P('dp', 'head'), may hold values from -300 to 300
- key_slots: bfloat16 [2, 2048, 8, 128], P('dp', 'head'), may hold values from -13 to 13
- value_slots: bfloat16 [2, 2048, 8, 128], P('dp', 'head'), may hold values from -5 to 5
- gate_logits: float32 [2, 2048, 8], P('dp', 'head'), may hold values from -8 to 310
- sink_logits: float32 [64], P('head'), may hold values from 1 to 6
- out_grad: bfloat16 [2, 2048, 8, 128], P('dp', 'head'), may hold values from -6 to 6
Outputs:
- mixed: bfloat16 [2, 2048, 8, 128], P('dp', 'head')
- query_grad: bfloat16 [2, 2048, 8, 128], P('dp', 'head')
- key_grad: bfloat16 [2, 2048, 8, 128], P('dp', 'head')
- value_grad: bfloat16 [2, 2048, 8, 128], P('dp', 'head')
- gate_grad: float32 [2, 2048, 8], P('dp', 'head')
- sink_grad: float32 [64], P('head')
Inputs may be any that keep to these rules, and one draw needn't show every extreme that they name: `head_ids`: each token names 8 different heads. Among the 128 tokens of one device no head is named more than 32 times, and in every group one head is named exactly 32 times by the tokens of every device of that group.
All inputs are finite; a program needn't handle non-finite values.
Results may differ from a plain program's by a relative error of at most 0.023.
Values may be sent and summed in bfloat16 or wider, within the bound.
No kernel may reach another device: no remote copies, remote signals or barrier semaphores. Data moves between devices by JAX's collectives and lax.ppermute only.
A program may use at most 64 MiB of HBM per device.

v0:
```python
import math
import jax
import jax.numpy as jnp
from jax import lax
from jax.sharding import PartitionSpec as P

HEADS = 64
BLOCK = 512
SLOT = 32
masked_value = -1e30


def block_scores(query_tile, key_tile, query_live, key_live, query_offset, key_offset, scale):
    scores = scale * jnp.einsum(
        "qd,kd->qk", query_tile, key_tile, preferred_element_type=jnp.float32
    )
    query_index = query_offset + lax.iota(jnp.int32, query_tile.shape[0])
    key_index = key_offset + lax.iota(jnp.int32, key_tile.shape[0])
    allowed = query_live[:, None] & key_live[None, :] & (key_index[None, :] <= query_index[:, None])
    return (scores, allowed)


def forward_head(query_rows, key_rows, value_rows, live_rows, sink_value, used_blocks, width):
    row_count, head_width = query_rows.shape
    scale = 1.0 / math.sqrt(head_width)

    def forward_query_block(qblock, carry):
        lse_all, out_all = carry
        offset = qblock * width
        query_tile = lax.dynamic_slice_in_dim(query_rows, offset, width, 0)
        query_live = lax.dynamic_slice_in_dim(live_rows, offset, width, 0)

        def tile_at(kblock):
            key_offset = kblock * width
            key_tile = lax.dynamic_slice_in_dim(key_rows, key_offset, width, 0)
            value_tile = lax.dynamic_slice_in_dim(value_rows, key_offset, width, 0)
            key_live = lax.dynamic_slice_in_dim(live_rows, key_offset, width, 0)
            scores, allowed = block_scores(
                query_tile, key_tile, query_live, key_live, offset, key_offset, scale
            )
            return (scores, allowed, value_tile)

        def stat_step(kblock, state):
            run_max, run_sum = state
            scores, allowed, value_tile = tile_at(kblock)
            masked = jnp.where(allowed, scores, masked_value)
            new_max = jnp.maximum(run_max, jnp.max(masked, axis=1))
            new_sum = run_sum * jnp.exp(run_max - new_max) + jnp.sum(
                jnp.where(allowed, jnp.exp(masked - new_max[:, None]), 0.0), axis=1
            )
            return (new_max, new_sum)

        start_state = (jnp.full((width,), sink_value, jnp.float32), jnp.ones((width,), jnp.float32))
        run_max, run_sum = lax.fori_loop(0, qblock + 1, stat_step, start_state)
        row_lse = run_max + jnp.log(run_sum)

        def value_step(kblock, total):
            scores, allowed, value_tile = tile_at(kblock)
            weights = jnp.where(allowed, jnp.exp(scores - row_lse[:, None]), 0.0).astype(
                jnp.bfloat16
            )
            return total + jnp.dot(weights, value_tile, preferred_element_type=jnp.float32)

        total = lax.fori_loop(
            0, qblock + 1, value_step, jnp.zeros((width, head_width), jnp.float32)
        )
        lse_all = lax.dynamic_update_slice_in_dim(lse_all, row_lse, offset, 0)
        out_all = lax.dynamic_update_slice_in_dim(out_all, total.astype(jnp.bfloat16), offset, 0)
        return (lse_all, out_all)

    start_all = (
        jnp.zeros((row_count,), jnp.float32),
        jnp.zeros((row_count, head_width), jnp.bfloat16),
    )
    return lax.fori_loop(0, used_blocks, forward_query_block, start_all)


def backward_head(
    query_rows,
    key_rows,
    value_rows,
    cot_rows,
    head_out,
    lse_all,
    live_rows,
    sink_value,
    used_blocks,
    width,
):
    row_count, head_width = query_rows.shape
    scale = 1.0 / math.sqrt(head_width)
    deltas = jnp.sum(cot_rows.astype(jnp.float32) * head_out.astype(jnp.float32), axis=1)
    sink_term = -jnp.sum(jnp.exp(sink_value - lse_all) * deltas)

    def backward_query_block(qblock, carry):
        qgrad_all, kgrad_acc, vgrad_acc = carry
        offset = qblock * width
        query_tile = lax.dynamic_slice_in_dim(query_rows, offset, width, 0)
        cot_tile = lax.dynamic_slice_in_dim(cot_rows, offset, width, 0)
        lse_tile = lax.dynamic_slice_in_dim(lse_all, offset, width, 0)
        delta_tile = lax.dynamic_slice_in_dim(deltas, offset, width, 0)
        query_live = lax.dynamic_slice_in_dim(live_rows, offset, width, 0)

        def key_step(kblock, inner):
            qgrad_run, kgrad_acc, vgrad_acc = inner
            key_offset = kblock * width
            key_tile = lax.dynamic_slice_in_dim(key_rows, key_offset, width, 0)
            value_tile = lax.dynamic_slice_in_dim(value_rows, key_offset, width, 0)
            key_live = lax.dynamic_slice_in_dim(live_rows, key_offset, width, 0)
            scores, allowed = block_scores(
                query_tile, key_tile, query_live, key_live, offset, key_offset, scale
            )
            probability = jnp.where(allowed, jnp.exp(scores - lse_tile[:, None]), 0.0)
            weights = probability.astype(jnp.bfloat16)
            dprob = jnp.einsum(
                "qd,kd->qk", cot_tile, value_tile, preferred_element_type=jnp.float32
            )
            dscore = (probability * (dprob - delta_tile[:, None])).astype(jnp.bfloat16)
            qgrad_run = qgrad_run + jnp.dot(dscore, key_tile, preferred_element_type=jnp.float32)
            kgrad_part = jnp.einsum(
                "qk,qd->kd", dscore, query_tile, preferred_element_type=jnp.float32
            )
            vgrad_part = jnp.einsum(
                "qk,qd->kd", weights, cot_tile, preferred_element_type=jnp.float32
            )
            kgrad_acc = lax.dynamic_update_slice_in_dim(
                kgrad_acc,
                lax.dynamic_slice_in_dim(kgrad_acc, key_offset, width, 0) + kgrad_part,
                key_offset,
                0,
            )
            vgrad_acc = lax.dynamic_update_slice_in_dim(
                vgrad_acc,
                lax.dynamic_slice_in_dim(vgrad_acc, key_offset, width, 0) + vgrad_part,
                key_offset,
                0,
            )
            return (qgrad_run, kgrad_acc, vgrad_acc)

        start_inner = (jnp.zeros((width, head_width), jnp.float32), kgrad_acc, vgrad_acc)
        qgrad_run, kgrad_acc, vgrad_acc = lax.fori_loop(0, qblock + 1, key_step, start_inner)
        qgrad_all = lax.dynamic_update_slice_in_dim(
            qgrad_all, (scale * qgrad_run).astype(jnp.bfloat16), offset, 0
        )
        return (qgrad_all, kgrad_acc, vgrad_acc)

    start_all = (
        jnp.zeros((row_count, head_width), jnp.bfloat16),
        jnp.zeros((row_count, head_width), jnp.float32),
        jnp.zeros((row_count, head_width), jnp.float32),
    )
    qgrad_all, kgrad_acc, vgrad_acc = lax.fori_loop(0, used_blocks, backward_query_block, start_all)
    return (
        qgrad_all,
        (scale * kgrad_acc).astype(jnp.bfloat16),
        vgrad_acc.astype(jnp.bfloat16),
        sink_term,
    )


def arrange(live_rows, width):
    row_count = live_rows.shape[0]
    return (None, None, row_count // width)


def pick_rows(buffer, head_slot):
    picked = buffer[:, head_slot].reshape(-1, buffer.shape[-1])
    return picked


def restore(row_block, devices):
    return row_block.reshape(devices, -1, row_block.shape[-1])


def per_device(head_ids, query_slots, key_slots, value_slots, gate_logits, sink_logits, out_grad):
    devices = lax.axis_size("head")
    local_heads = HEADS // devices
    selected = head_ids[0]
    token_count, slot_count = selected.shape
    head_width = query_slots.shape[-1]
    matches = (selected[:, :, None] == lax.iota(jnp.int32, HEADS)[None, None, :]).astype(jnp.int32)
    per_token = jnp.sum(matches, axis=1)
    earlier = jnp.cumsum(per_token, axis=0) - per_token
    placing = jnp.sum(matches * earlier[:, None, :], axis=2)
    target = (selected * SLOT + placing).reshape(-1)
    buffer_rows = HEADS * SLOT

    def spread_out(flat_rows):
        filled_rows = (
            jnp.zeros((buffer_rows, flat_rows.shape[-1]), flat_rows.dtype).at[target].set(flat_rows)
        )
        return filled_rows.reshape(devices, local_heads, SLOT, flat_rows.shape[-1])

    def collect(buffer):
        return buffer.reshape(buffer_rows, buffer.shape[-1])[target].reshape(
            token_count, slot_count, buffer.shape[-1]
        )

    gate_probs = jax.nn.softmax(gate_logits[0], axis=-1)
    cotangent = (gate_probs[:, :, None] * out_grad[0].astype(jnp.float32)).astype(jnp.bfloat16)
    send_query = spread_out(query_slots[0].reshape(-1, head_width))
    send_key = spread_out(key_slots[0].reshape(-1, head_width))
    send_value = spread_out(value_slots[0].reshape(-1, head_width))
    send_cot = spread_out(cotangent.reshape(-1, head_width))
    filled = (
        jnp.zeros((buffer_rows,), jnp.bfloat16)
        .at[target]
        .set(jnp.ones((), jnp.bfloat16))
        .reshape(devices, local_heads, SLOT)
    )
    out_list, qgrad_list, kgrad_list, vgrad_list, sink_list = ([], [], [], [], [])
    recv_query, recv_key, recv_value, recv_fill = (
        lax.all_to_all(send_query, "head", split_axis=0, concat_axis=0, tiled=True),
        lax.all_to_all(send_key, "head", split_axis=0, concat_axis=0, tiled=True),
        lax.all_to_all(send_value, "head", split_axis=0, concat_axis=0, tiled=True),
        lax.all_to_all(filled, "head", split_axis=0, concat_axis=0, tiled=True),
    )
    prepared = []
    lse_list = []
    head_outs = []
    for head_slot in range(local_heads):
        live_rows = recv_fill[:, head_slot].reshape(-1) > 0
        gather_order, landing, used_blocks = arrange(live_rows, BLOCK)
        live_use = live_rows
        pieces = (
            pick_rows(recv_query, head_slot),
            pick_rows(recv_key, head_slot),
            pick_rows(recv_value, head_slot),
        )
        pieces, live_use, gather_order, landing, used_blocks = (
            pieces,
            live_use,
            gather_order,
            landing,
            used_blocks,
        )
        row_lse, head_out = forward_head(
            pieces[0], pieces[1], pieces[2], live_use, sink_logits[head_slot], used_blocks, BLOCK
        )
        prepared.append((pieces, live_use, gather_order, landing, used_blocks))
        lse_list.append(row_lse)
        head_outs.append(head_out)
        out_list.append(restore(head_out, devices))
    back_out = lax.all_to_all(
        jnp.stack(out_list, axis=1), "head", split_axis=0, concat_axis=0, tiled=True
    )
    recv_cot = lax.all_to_all(send_cot, "head", split_axis=0, concat_axis=0, tiled=True)
    for head_slot in range(local_heads):
        pieces, live_use, gather_order, landing, used_blocks = prepared[head_slot]
        cot_rows = pick_rows(recv_cot, head_slot)
        qgrad, kgrad, vgrad, sink_term = backward_head(
            pieces[0],
            pieces[1],
            pieces[2],
            cot_rows,
            head_outs[head_slot],
            lse_list[head_slot],
            live_use,
            sink_logits[head_slot],
            used_blocks,
            BLOCK,
        )
        qgrad_list.append(restore(qgrad, devices))
        kgrad_list.append(restore(kgrad, devices))
        vgrad_list.append(restore(vgrad, devices))
        sink_list.append(sink_term)
    back_qgrad, back_kgrad, back_vgrad = (
        lax.all_to_all(
            jnp.stack(qgrad_list, axis=1), "head", split_axis=0, concat_axis=0, tiled=True
        ),
        lax.all_to_all(
            jnp.stack(kgrad_list, axis=1), "head", split_axis=0, concat_axis=0, tiled=True
        ),
        lax.all_to_all(
            jnp.stack(vgrad_list, axis=1), "head", split_axis=0, concat_axis=0, tiled=True
        ),
    )
    sink_grad = lax.psum(jnp.stack(sink_list), "dp")
    token_out = collect(back_out).astype(jnp.float32)
    mixed = (gate_probs[:, :, None] * token_out).astype(jnp.bfloat16)
    gate_sum = jnp.sum(out_grad[0].astype(jnp.float32) * token_out, axis=-1)
    gate_grad = gate_probs * (gate_sum - jnp.sum(gate_probs * gate_sum, axis=-1, keepdims=True))
    return (
        mixed[None],
        collect(back_qgrad)[None],
        collect(back_kgrad)[None],
        collect(back_vgrad)[None],
        gate_grad[None],
        sink_grad,
    )


def solution(mesh):
    placed = (
        P("dp", "head", None),
        P("dp", "head", None, None),
        P("dp", "head", None, None),
        P("dp", "head", None, None),
        P("dp", "head", None),
        P("head"),
        P("dp", "head", None, None),
    )
    return jax.shard_map(
        per_device,
        mesh=mesh,
        in_specs=placed,
        out_specs=(
            P("dp", "head", None, None),
            P("dp", "head", None, None),
            P("dp", "head", None, None),
            P("dp", "head", None, None),
            P("dp", "head", None),
            P("head"),
        ),
        check_vma=False,
    )
```

profile of v0, /device:TPU:0, one launch (start us, length us, event | category | flops | bytes accessed | tf_op | source)
XLA Modules:
  0.0 204.0 jit_solution(5614113830701706993)
XLA Ops:
  0.7 0.8 broadcast_multiply_fusion
  2.3 7.6 %scatter_custom_fusion = bf16[2048]{0:T(1024)(128)(2,1)S(1)} fusion(s32[1024]{0:T(1024)S(1)} %bitcast.236, bf16[1024]{0:T(1024)(128)(2,1)S(1)} %broadcast.376, bf16[]{:T(256)} %constant.402.clone.1), kind=kCustom, calls=%fused_computation.130 | custom fusion | bytes 4098 | tf_op jit(solution)/shard_map/scatter | solution.py:208
  9.9 0.7 reshape.293
  10.6 7.4 %all-to-all-start = ((bf16[16,4,32]{2,1,0:T(4,128)(2,1)}), bf16[16,4,32]{2,1,0:T(4,128)(2,1)S(1)}, u32[]{:S(2)}, u32[]{:S(2)}) async-start(bf16[16,4,32]{2,1,0:T(4,128)(2,1)} %reshape.293), calls=%async_computation | async-start | bytes 32768 | tf_op jit(solution)/shard_map/all_to_all | solution.py:216
  18.0 4.0 %scatter_custom_fusion.2 = bf16[2048,128]{1,0:T(8,128)(2,1)} fusion(s32[1024]{0:T(1024)S(1)} %bitcast.237, bf16[1,128,8,128]{3,2,1,0:T(8,128)(2,1)S(1)} %copy-done, bf16[]{:T(256)} %constant.402.clone.1), kind=kCustom, calls=%fused_computation.91 | custom fusion | bytes 786434 | tf_op jit(solution)/shard_map/scatter | solution.py:190
  22.0 2.5 %all-to-all-done = bf16[16,4,32]{2,1,0:T(4,128)(2,1)S(1)} async-done(((bf16[16,4,32]{2,1,0:T(4,128)(2,1)}), bf16[16,4,32]{2,1,0:T(4,128)(2,1)S(1)}, u32[]{:S(2)}, u32[]{:S(2)}) %all-to-all-start) | async-done | bytes 4128 | tf_op jit(solution)/shard_map/all_to_all | solution.py:216
  24.5 3.7 %all-to-all-start.2 = ((bf16[16,4,32,128]{3,2,1,0:T(8,128)(2,1)}), bf16[16,4,32,128]{3,2,1,0:T(8,128)(2,1)S(1)}, u32[]{:S(2)}, u32[]{:S(2)}) async-start(bf16[16,4,32,128]{3,2,1,0:T(8,128)(2,1)} %bitcast.7), calls=%async_computation.2 | async-start | bytes 1048576 | tf_op jit(solution)/shard_map/all_to_all | solution.py:214
  28.2 4.0 %scatter_custom_fusion.1 = bf16[2048,128]{1,0:T(8,128)(2,1)} fusion(s32[1024]{0:T(1024)S(1)} %bitcast.238, bf16[1,128,8,128]{3,2,1,0:T(8,128)(2,1)S(1)} %copy-done.18, bf16[]{:T(256)} %constant.402.clone.1), kind=kCustom, calls=%fused_computation.93 | custom fusion | bytes 786434 | tf_op jit(solution)/shard_map/scatter | solution.py:190
  32.2 10.2 %all-to-all-done.2 = bf16[16,4,32,128]{3,2,1,0:T(8,128)(2,1)S(1)} async-done(((bf16[16,4,32,128]{3,2,1,0:T(8,128)(2,1)}), bf16[16,4,32,128]{3,2,1,0:T(8,128)(2,1)S(1)}, u32[]{:S(2)}, u32[]{:S(2)}) %all-to-all-start.2) | async-done | bytes 524320 | tf_op jit(solution)/shard_map/all_to_all | solution.py:214
  42.4 4.3 %all-to-all-start.1 = ((bf16[16,4,32,128]{3,2,1,0:T(8,128)(2,1)}), bf16[16,4,32,128]{3,2,1,0:T(8,128)(2,1)S(1)}, u32[]{:S(2)}, u32[]{:S(2)}) async-start(bf16[16,4,32,128]{3,2,1,0:T(8,128)(2,1)} %bitcast.4), calls=%async_computation.1 | async-start | bytes 1048576 | tf_op jit(solution)/shard_map/all_to_all | solution.py:213
  47.6 4.5 %scatter_custom_fusion.4 = bf16[2048,128]{1,0:T(8,128)(2,1)} fusion(s32[1024]{0:T(1024)S(1)} %bitcast.239, bf16[1,128,8,128]{3,2,1,0:T(8,128)(2,1)S(1)} %copy-done.4, f32[1024]{0:T(1024)S(1)} %exponential_divide_fusion, bf16[]{:T(256)} %constant.402.clone.1), kind=kCustom, calls=%fused_computation.88 | custom fusion | flops 393216 | bytes 790530 | tf_op jit(solution)/shard_map/scatter | solution.py:190
  52.1 8.8 %all-to-all-done.1 = bf16[16,4,32,128]{3,2,1,0:T(8,128)(2,1)S(1)} async-done(((bf16[16,4,32,128]{3,2,1,0:T(8,128)(2,1)}), bf16[16,4,32,128]{3,2,1,0:T(8,128)(2,1)S(1)}, u32[]{:S(2)}, u32[]{:S(2)}) %all-to-all-start.1) | async-done | bytes 524320 | tf_op jit(solution)/shard_map/all_to_all | solution.py:213
  61.0 4.3 %all-to-all-start.5 = ((bf16[16,4,32,128]{3,2,1,0:T(8,128)(2,1)}), bf16[16,4,32,128]{3,2,1,0:T(8,128)(2,1)S(1)}, u32[]{:S(2)}, u32[]{:S(2)}) async-start(bf16[16,4,32,128]{3,2,1,0:T(8,128)(2,1)} %bitcast.36), calls=%async_computation.5 | async-start | bytes 1048576 | tf_op jit(solution)/shard_map/all_to_all | solution.py:247
  65.3 4.0 %scatter_custom_fusion.3 = bf16[2048,128]{1,0:T(8,128)(2,1)} fusion(s32[1024]{0:T(1024)S(1)} %bitcast.240, bf16[1,128,8,128]{3,2,1,0:T(8,128)(2,1)S(1)} %copy-done.19, bf16[]{:T(256)} %constant.402.clone.1), kind=kCustom, calls=%fused_computation.89 | custom fusion | bytes 786434 | tf_op jit(solution)/shard_map/scatter | solution.py:190
  69.3 0.6 fusion.66
  70.4 0.7 fusion.63
  71.1 0.8 fusion.64
  72.3 7.3 %all-to-all-done.5 = bf16[16,4,32,128]{3,2,1,0:T(8,128)(2,1)S(1)} async-done(((bf16[16,4,32,128]{3,2,1,0:T(8,128)(2,1)}), bf16[16,4,32,128]{3,2,1,0:T(8,128)(2,1)S(1)}, u32[]{:S(2)}, u32[]{:S(2)}) %all-to-all-start.5) | async-done | bytes 524320 | tf_op jit(solution)/shard_map/all_to_all | solution.py:247
  79.5 4.2 %all-to-all-start.3 = ((bf16[16,4,32,128]{3,2,1,0:T(8,128)(2,1)}), bf16[16,4,32,128]{3,2,1,0:T(8,128)(2,1)S(1)}, u32[]{:S(2)}, u32[]{:S(2)}) async-start(bf16[16,4,32,128]{3,2,1,0:T(8,128)(2,1)} %bitcast.11), calls=%async_computation.3 | async-start | bytes 1048576 | tf_op jit(solution)/shard_map/all_to_all | solution.py:215
  83.7 0.6 broadcast_maximum_fusion
  84.6 0.6 log_add_fusion
  85.2 0.7 fusion.62
  86.2 11.8 %all-to-all-done.3 = bf16[16,4,32,128]{3,2,1,0:T(8,128)(2,1)S(1)} async-done(((bf16[16,4,32,128]{3,2,1,0:T(8,128)(2,1)}), bf16[16,4,32,128]{3,2,1,0:T(8,128)(2,1)S(1)}, u32[]{:S(2)}, u32[]{:S(2)}) %all-to-all-start.3) | async-done | bytes 524320 | tf_op jit(solution)/shard_map/all_to_all | solution.py:215
  98.0 0.7 fusion.65
  98.7 1.1 multiply_reduce_fusion
  100.1 0.9 fusion.15
  101.4 0.7 broadcast_maximum_fusion.3
  102.4 0.7 log_add_fusion.3
  103.4 1.1 multiply_reduce_fusion.3
  104.5 1.3 fusion.7
  105.8 0.9 fusion.12
  107.1 0.7 broadcast_maximum_fusion.1
  108.1 0.7 log_add_fusion.1
  109.1 1.1 multiply_reduce_fusion.1
  111.5 0.7 broadcast_maximum_fusion.2
  112.5 0.7 log_add_fusion.2
  113.5 0.9 pad_maximum_fusion.3
  114.4 4.2 %all-to-all-start.8 = ((bf16[16,4,32,128]{3,2,1,0:T(8,128)(2,1)}), bf16[16,4,32,128]{3,2,1,0:T(8,128)(2,1)S(1)}, u32[]{:S(2)}, u32[]{:S(2)}) async-start(bf16[16,4,32,128]{3,2,1,0:T(8,128)(2,1)} %pad_maximum_fusion.3), calls=%async_computation.8 | async-start | bytes 1048576 | tf_op jit(solution)/shard_map/all_to_all | solution.py:274
  118.6 1.2 fusion.14
  119.9 1.1 multiply_reduce_fusion.2
  121.0 1.6 fusion.6
  123.0 0.7 copy-done.16
  123.8 0.9 pad_maximum_fusion.2
  124.7 8.2 %all-to-all-done.8 = bf16[16,4,32,128]{3,2,1,0:T(8,128)(2,1)S(1)} async-done(((bf16[16,4,32,128]{3,2,1,0:T(8,128)(2,1)}), bf16[16,4,32,128]{3,2,1,0:T(8,128)(2,1)S(1)}, u32[]{:S(2)}, u32[]{:S(2)}) %all-to-all-start.8) | async-done | bytes 524320 | tf_op jit(solution)/shard_map/all_to_all | solution.py:274
  132.9 4.2 %all-to-all-start.7 = ((bf16[16,4,32,128]{3,2,1,0:T(8,128)(2,1)}), bf16[16,4,32,128]{3,2,1,0:T(8,128)(2,1)S(1)}, u32[]{:S(2)}, u32[]{:S(2)}) async-start(bf16[16,4,32,128]{3,2,1,0:T(8,128)(2,1)} %pad_maximum_fusion.2), calls=%async_computation.7 | async-start | bytes 1048576 | tf_op jit(solution)/shard_map/all_to_all | solution.py:271
  137.1 0.9 pad_maximum_fusion
  138.0 13.4 %all-to-all-done.7 = bf16[16,4,32,128]{3,2,1,0:T(8,128)(2,1)S(1)} async-done(((bf16[16,4,32,128]{3,2,1,0:T(8,128)(2,1)}), bf16[16,4,32,128]{3,2,1,0:T(8,128)(2,1)S(1)}, u32[]{:S(2)}, u32[]{:S(2)}) %all-to-all-start.7) | async-done | bytes 524320 | tf_op jit(solution)/shard_map/all_to_all | solution.py:271
  151.3 4.2 %all-to-all-start.4 = ((bf16[16,4,32,128]{3,2,1,0:T(8,128)(2,1)}), bf16[16,4,32,128]{3,2,1,0:T(8,128)(2,1)S(1)}, u32[]{:S(2)}, u32[]{:S(2)}) async-start(bf16[16,4,32,128]{3,2,1,0:T(8,128)(2,1)} %pad_maximum_fusion), calls=%async_computation.4 | async-start | bytes 1048576 | tf_op jit(solution)/shard_map/all_to_all | solution.py:244
  155.5 1.3 fusion.11
  156.8 1.2 multiply_reduce_fusion.5
  159.2 0.7 copy-done.2
  160.3 0.9 pad_maximum_fusion.1
  161.1 8.6 %all-to-all-done.4 = bf16[16,4,32,128]{3,2,1,0:T(8,128)(2,1)S(1)} async-done(((bf16[16,4,32,128]{3,2,1,0:T(8,128)(2,1)}), bf16[16,4,32,128]{3,2,1,0:T(8,128)(2,1)S(1)}, u32[]{:S(2)}, u32[]{:S(2)}) %all-to-all-start.4) | async-done | bytes 524320 | tf_op jit(solution)/shard_map/all_to_all | solution.py:244
  169.8 4.2 %all-to-all-start.6 = ((bf16[16,4,32,128]{3,2,1,0:T(8,128)(2,1)}), bf16[16,4,32,128]{3,2,1,0:T(8,128)(2,1)S(1)}, u32[]{:S(2)}, u32[]{:S(2)}) async-start(bf16[16,4,32,128]{3,2,1,0:T(8,128)(2,1)} %pad_maximum_fusion.1), calls=%async_computation.6 | async-start | bytes 1048576 | tf_op jit(solution)/shard_map/all_to_all | solution.py:268
  173.9 1.3 multiply_reduce_fusion.8
  176.5 1.3 multiply_reduce_fusion.6
  178.4 1.3 multiply_reduce_fusion.7
  180.4 5.4 %psum.7 = f32[4]{0:T(128)} all-reduce(f32[4]{0:T(128)S(1)} %pad_maximum_fusion.4), channel_id=1, replica_groups=mesh['dp'=2,'head'=16] {'dp'}, use_global_device_ids=true, to_apply=%region_28.29 | all-reduce | flops 4 | bytes 32 | tf_op jit(solution)/shard_map/psum | solution.py:278
  185.8 4.3 %gather_fusion.3 = bf16[1024,128]{1,0:T(8,128)(2,1)} fusion(bf16[2048,128]{1,0:T(8,128)(2,1)S(1)} %bitcast.179, s32[1024]{0:T(1024)S(1)} %broadcast_clamp_fusion), kind=kCustom, calls=%fused_computation.3 | custom fusion | bytes 528384 | tf_op jit(solution)/shard_map/gather | solution.py:195
  190.1 4.3 %gather_fusion.2 = bf16[1024,128]{1,0:T(8,128)(2,1)} fusion(bf16[2048,128]{1,0:T(8,128)(2,1)S(1)} %bitcast.180, s32[1024]{0:T(1024)S(1)} %broadcast_clamp_fusion), kind=kCustom, calls=%fused_computation.2 | custom fusion | bytes 528384 | tf_op jit(solution)/shard_map/gather | solution.py:195
  194.4 3.2 %gather_fusion = bf16[1024,128]{1,0:T(8,128)(2,1)S(1)} fusion(bf16[2048,128]{1,0:T(8,128)(2,1)S(1)} %bitcast.181, s32[1024]{0:T(1024)S(1)} %broadcast_clamp_fusion), kind=kCustom, calls=%fused_computation | custom fusion | bytes 528384 | tf_op jit(solution)/shard_map/gather | solution.py:195
  198.1 4.3 %gather_fusion.1 = bf16[1024,128]{1,0:T(8,128)(2,1)} fusion(bf16[2048,128]{1,0:T(8,128)(2,1)S(1)} %bitcast.182, s32[1024]{0:T(1024)S(1)} %broadcast_clamp_fusion), kind=kCustom, calls=%fused_computation.1 | custom fusion | bytes 528384 | tf_op jit(solution)/shard_map/gather | solution.py:195
  202.5 0.9 fusion.25
  203.4 0.6 fusion.50
  (110 shorter events, 10.2 us)
Async XLA Ops:
  0.6 17.3 %copy-start = (bf16[1,128,8,128]{3,2,1,0:T(8,128)(2,1)S(1)}, bf16[1,128,8,128]{3,2,1,0:T(8,128)(2,1)}, u32[]{:S(2)}) copy-start(bf16[1,128,8,128]{3,2,1,0:T(8,128)(2,1)} %param.9) | copy-start | bytes 786436
  0.6 0.8 copy-start.29
  10.6 13.9 %all-to-all-start = ((bf16[16,4,32]{2,1,0:T(4,128)(2,1)}), bf16[16,4,32]{2,1,0:T(4,128)(2,1)S(1)}, u32[]{:S(2)}, u32[]{:S(2)}) async-start(bf16[16,4,32]{2,1,0:T(4,128)(2,1)} %reshape.293), calls=%async_computation | async-start | bytes 32768 | tf_op jit(solution)/shard_map/all_to_all | solution.py:216
  24.5 3.7 %copy-start.18 = (bf16[1,128,8,128]{3,2,1,0:T(8,128)(2,1)S(1)}, bf16[1,128,8,128]{3,2,1,0:T(8,128)(2,1)}, u32[]{:S(2)}) copy-start(bf16[1,128,8,128]{3,2,1,0:T(8,128)(2,1)} %param.8) | copy-start | bytes 786436
  24.5 17.9 %all-to-all-start.2 = ((bf16[16,4,32,128]{3,2,1,0:T(8,128)(2,1)}), bf16[16,4,32,128]{3,2,1,0:T(8,128)(2,1)S(1)}, u32[]{:S(2)}, u32[]{:S(2)}) async-start(bf16[16,4,32,128]{3,2,1,0:T(8,128)(2,1)} %bitcast.7), calls=%async_computation.2 | async-start | bytes 1048576 | tf_op jit(solution)/shard_map/all_to_all | solution.py:214
  42.4 4.3 %copy-start.28 = (f32[1,128,8]{1,2,0:T(8,128)S(1)}, f32[1,128,8]{1,2,0:T(8,128)}, u32[]{:S(2)}) copy-start(f32[1,128,8]{1,2,0:T(8,128)} %param.11) | copy-start | bytes 12292
  42.4 18.5 %all-to-all-start.1 = ((bf16[16,4,32,128]{3,2,1,0:T(8,128)(2,1)}), bf16[16,4,32,128]{3,2,1,0:T(8,128)(2,1)S(1)}, u32[]{:S(2)}, u32[]{:S(2)}) async-start(bf16[16,4,32,128]{3,2,1,0:T(8,128)(2,1)} %bitcast.4), calls=%async_computation.1 | async-start | bytes 1048576 | tf_op jit(solution)/shard_map/all_to_all | solution.py:213
  46.7 1.0 copy-start.4
  61.0 4.3 %copy-start.19 = (bf16[1,128,8,128]{3,2,1,0:T(8,128)(2,1)S(1)}, bf16[1,128,8,128]{3,2,1,0:T(8,128)(2,1)}, u32[]{:S(2)}) copy-start(bf16[1,128,8,128]{3,2,1,0:T(8,128)(2,1)} %param.10) | copy-start | bytes 786436
  61.0 18.6 %all-to-all-start.5 = ((bf16[16,4,32,128]{3,2,1,0:T(8,128)(2,1)}), bf16[16,4,32,128]{3,2,1,0:T(8,128)(2,1)S(1)}, u32[]{:S(2)}, u32[]{:S(2)}) async-start(bf16[16,4,32,128]{3,2,1,0:T(8,128)(2,1)} %bitcast.36), calls=%async_computation.5 | async-start | bytes 1048576 | tf_op jit(solution)/shard_map/all_to_all | solution.py:247
  65.3 4.0 %copy-start.30 = (f32[4]{0:T(128)S(1)}, f32[4]{0:T(128)}, u32[]{:S(2)}) copy-start(f32[4]{0:T(128)} %param.12) | copy-start | bytes 52
  71.1 0.8 copy-start.12
  71.1 30.0 %copy-start.10 = (bf16[16,1,32,128]{3,2,1,0:T(8,128)(2,1)}, bf16[16,1,32,128]{3,2,1,0:T(8,128)(2,1)S(1)}, u32[]{:S(2)}) copy-start(bf16[16,1,32,128]{3,2,1,0:T(8,128)(2,1)S(1)} %get-tuple-element.1312) | copy-start | bytes 393220
  71.1 35.6 %copy-start.8 = (bf16[16,1,32,128]{3,2,1,0:T(8,128)(2,1)}, bf16[16,1,32,128]{3,2,1,0:T(8,128)(2,1)S(1)}, u32[]{:S(2)}) copy-start(bf16[16,1,32,128]{3,2,1,0:T(8,128)(2,1)S(1)} %get-tuple-element.1314) | copy-start | bytes 393220
  71.9 34.8 %copy-start.15 = (bf16[16,1,32,128]{3,2,1,0:T(8,128)(2,1)}, bf16[16,1,32,128]{3,2,1,0:T(8,128)(2,1)S(1)}, u32[]{:S(2)}) copy-start(bf16[16,1,32,128]{3,2,1,0:T(8,128)(2,1)S(1)} %get-tuple-element.1318) | copy-start | bytes 393220
  79.5 18.4 %all-to-all-start.3 = ((bf16[16,4,32,128]{3,2,1,0:T(8,128)(2,1)}), bf16[16,4,32,128]{3,2,1,0:T(8,128)(2,1)S(1)}, u32[]{:S(2)}, u32[]{:S(2)}) async-start(bf16[16,4,32,128]{3,2,1,0:T(8,128)(2,1)} %bitcast.11), calls=%async_computation.3 | async-start | bytes 1048576 | tf_op jit(solution)/shard_map/all_to_all | solution.py:215
  85.9 17.6 %copy-start.26 = (bf16[16,1,32,128]{3,2,1,0:T(8,128)(2,1)}, bf16[16,1,32,128]{3,2,1,0:T(8,128)(2,1)S(1)}, u32[]{:S(2)}) copy-start(bf16[16,1,32,128]{3,2,1,0:T(8,128)(2,1)S(1)} %get-tuple-element.1308) | copy-start | bytes 393220
  110.2 0.9 copy-start.6
  110.2 1.0 copy-start.13
  111.5 8.4 %copy-start.3 = (f32[512,512]{0,1:T(8,128)}, f32[512,512]{0,1:T(8,128)S(1)}, u32[]{:S(2)}) copy-start(f32[512,512]{0,1:T(8,128)S(1)} %get-tuple-element.1333) | copy-start | bytes 3145732
  112.2 1.0 copy-start.21
  114.4 18.4 %all-to-all-start.8 = ((bf16[16,4,32,128]{3,2,1,0:T(8,128)(2,1)}), bf16[16,4,32,128]{3,2,1,0:T(8,128)(2,1)S(1)}, u32[]{:S(2)}, u32[]{:S(2)}) async-start(bf16[16,4,32,128]{3,2,1,0:T(8,128)(2,1)} %pad_maximum_fusion.3), calls=%async_computation.8 | async-start | bytes 1048576 | tf_op jit(solution)/shard_map/all_to_all | solution.py:274
  118.6 1.3 copy-start.22
  118.6 1.3 copy-start.24
  121.0 1.6 copy-start.14
  122.6 2.0 %copy-start.1 = (bf16[512,512]{0,1:T(8,128)(2,1)}, bf16[512,512]{0,1:T(8,128)(2,1)S(1)}, u32[]{:S(2)}) copy-start(bf16[512,512]{0,1:T(8,128)(2,1)S(1)} %fusion.6) | copy-start | bytes 1572868
  122.7 1.0 copy-start.16
  122.7 1.1 copy-start.17
  124.7 12.4 %copy-start.20 = (bf16[512,128]{1,0:T(8,128)(2,1)S(1)}, bf16[512,128]{1,0:T(8,128)(2,1)}, u32[]{:S(2)}) copy-start(bf16[512,128]{1,0:T(8,128)(2,1)} %get-tuple-element.1337) | copy-start | bytes 393220
  124.7 12.4 %copy-start.23 = (bf16[512,128]{1,0:T(8,128)(2,1)S(1)}, bf16[512,128]{1,0:T(8,128)(2,1)}, u32[]{:S(2)}) copy-start(bf16[512,128]{1,0:T(8,128)(2,1)} %get-tuple-element.1343) | copy-start | bytes 393220
  124.7 12.4 %copy-start.25 = (bf16[512,128]{1,0:T(8,128)(2,1)S(1)}, bf16[512,128]{1,0:T(8,128)(2,1)}, u32[]{:S(2)}) copy-start(bf16[512,128]{1,0:T(8,128)(2,1)} %get-tuple-element.1339) | copy-start | bytes 393220
  124.7 12.4 %copy-start.27 = (bf16[512,128]{1,0:T(8,128)(2,1)S(1)}, bf16[512,128]{1,0:T(8,128)(2,1)}, u32[]{:S(2)}) copy-start(bf16[512,128]{1,0:T(8,128)(2,1)} %get-tuple-element.1341) | copy-start | bytes 393220
  132.9 18.4 %all-to-all-start.7 = ((bf16[16,4,32,128]{3,2,1,0:T(8,128)(2,1)}), bf16[16,4,32,128]{3,2,1,0:T(8,128)(2,1)S(1)}, u32[]{:S(2)}, u32[]{:S(2)}) async-start(bf16[16,4,32,128]{3,2,1,0:T(8,128)(2,1)} %pad_maximum_fusion.2), calls=%async_computation.7 | async-start | bytes 1048576 | tf_op jit(solution)/shard_map/all_to_all | solution.py:271
  151.3 18.4 %all-to-all-start.4 = ((bf16[16,4,32,128]{3,2,1,0:T(8,128)(2,1)}), bf16[16,4,32,128]{3,2,1,0:T(8,128)(2,1)S(1)}, u32[]{:S(2)}, u32[]{:S(2)}) async-start(bf16[16,4,32,128]{3,2,1,0:T(8,128)(2,1)} %pad_maximum_fusion), calls=%async_computation.4 | async-start | bytes 1048576 | tf_op jit(solution)/shard_map/all_to_all | solution.py:244
  155.5 2.5 %copy-start.11 = (bf16[16,1,32,128]{3,2,1,0:T(8,128)(2,1)S(1)}, bf16[16,1,32,128]{3,2,1,0:T(8,128)(2,1)}, u32[]{:S(2)}) copy-start(bf16[16,1,32,128]{3,2,1,0:T(8,128)(2,1)} %copy-done.10) | copy-start | bytes 393220
  158.0 0.9 copy-start.9
  158.9 1.0 copy-start.2
  158.9 1.1 copy-start.7
  169.8 28.4 %all-to-all-start.6 = ((bf16[16,4,32,128]{3,2,1,0:T(8,128)(2,1)}), bf16[16,4,32,128]{3,2,1,0:T(8,128)(2,1)S(1)}, u32[]{:S(2)}, u32[]{:S(2)}) async-start(bf16[16,4,32,128]{3,2,1,0:T(8,128)(2,1)} %pad_maximum_fusion.1), calls=%async_computation.6 | async-start | bytes 1048576 | tf_op jit(solution)/shard_map/all_to_all | solution.py:268
  194.4 3.2 %copy-start.5 = (bf16[1,128,8,128]{3,2,1,0:T(8,128)(2,1)S(1)}, bf16[1,128,8,128]{3,2,1,0:T(8,128)(2,1)}, u32[]{:S(2)}) copy-start(bf16[1,128,8,128]{3,2,1,0:T(8,128)(2,1)} %param.13) | copy-start | bytes 786436
where the time goes:
time: 205 us; the launch traced here: 204 us
  waiting for transfers between devices  70.8 us (35%)
  local copies, waits for them, and re-layouts  44.4 us (22%)
  starting transfers between devices  40.5 us (20%)
  other arithmetic  22.6 us (11%)
  matrix products  16.5 us (8%)
  blocking collectives  5.42 us (3%)
  between operations  3.8 us (2%)
    gather x4, local copies, waits for them, and re-layouts, collect(): buffer.reshape(buffer_rows, buffer.shape[-1])[target]  16.1 us
    all_to_all x1, waiting for transfers between devices, per_device(): lax.all_to_all(jnp.stack(kgrad_list, axis=1), 'head', split_axis=0, conca...  13.4 us
    scatter x3, local copies, waits for them, and re-layouts, spread_out(): jnp.zeros((buffer_rows, flat_rows.shape[-1]), flat_rows.dtype).at[target]  12 us
    all_to_all x1, waiting for transfers between devices, per_device(): lax.all_to_all(send_value, 'head', split_axis=0, concat_axis=0, tiled=True)  11.8 us
    all_to_all x1, waiting for transfers between devices, per_device(): lax.all_to_all(send_key, 'head', split_axis=0, concat_axis=0, tiled=True)  10.2 us
    all_to_all x1, waiting for transfers between devices, per_device(): lax.all_to_all(send_query, 'head', split_axis=0, concat_axis=0, tiled=True)  8.84 us
    all_to_all x1, waiting for transfers between devices, per_device(): lax.all_to_all(jnp.stack(out_list, axis=1), 'head', split_axis=0, concat_...  8.62 us
    all_to_all x1, waiting for transfers between devices, per_device(): lax.all_to_all(jnp.stack(vgrad_list, axis=1), 'head', split_axis=0, conca...  8.16 us
  transfers between devices with their start and end apart: 9, of which 8 were waited for; matrix products, arithmetic and copies ran while one was open for 24% of the time, Pallas kernels for 0%

commit v1 on v0

--- a/solution.py
+++ b/solution.py
@@ -8,6 +8,18 @@
 BLOCK = 512
 SLOT = 32
 masked_value = -1e30
+
+
+def exchange_directly(shard, axis, split, join):
+    ways, here = (lax.axis_size(axis), lax.axis_index(axis))
+    width = shard.shape[split] // ways
+    turned = jnp.roll(shard, -here * width, axis=split)
+    got = [lax.slice_in_dim(turned, 0, width, axis=split)]
+    for far in range(1, ways):
+        sent = lax.slice_in_dim(turned, far * width, (far + 1) * width, axis=split)
+        got.append(lax.ppermute(sent, axis, [(d, (d + far) % ways) for d in range(ways)]))
+    line = jnp.concatenate(got[::-1], axis=join)
+    return jnp.roll(line, (here + 1) * got[0].shape[join], axis=join)
 
 
 def block_scores(query_tile, key_tile, query_live, key_live, query_offset, key_offset, scale):
@@ -210,7 +222,7 @@
     )
     out_list, qgrad_list, kgrad_list, vgrad_list, sink_list = ([], [], [], [], [])
     recv_query, recv_key, recv_value, recv_fill = (
-        lax.all_to_all(send_query, "head", split_axis=0, concat_axis=0, tiled=True),
+        exchange_directly(send_query, "head", 0, 0),
         lax.all_to_all(send_key, "head", split_axis=0, concat_axis=0, tiled=True),
         lax.all_to_all(send_value, "head", split_axis=0, concat_axis=0, tiled=True),
         lax.all_to_all(filled, "head", split_axis=0, concat_axis=0, tiled=True),

time: 205 us -> 251 us (1.22)
  starting transfers between devices: 40.5 us -> 78.4 us
  waiting for transfers between devices: 70.8 us -> 76.2 us
    ppermute x0 -> x15, starting transfers between devices: none -> 40.5 us  [exchange_directly(): lax.ppermute(sent, axis, [(d, (d + far) % ways) for d in range(ways)])]
    ppermute x0 -> x15, waiting for transfers between devices: none -> 23.4 us  [exchange_directly(): lax.ppermute(sent, axis, [(d, (d + far) % ways) for d in range(ways)])]
    all_to_all x1, waiting for transfers between devices: 10.2 us -> 0.01 us  [per_device(): lax.all_to_all(send_key, 'head', split_axis=0, concat_axis=0, tiled=True)]
    all_to_all x1 -> x0, waiting for transfers between devices: 8.84 us -> none  [per_device(): lax.all_to_all(send_query, 'head', split_axis=0, concat_axis=0, tiled=True)]
    all_to_all x1, waiting for transfers between devices: 7.28 us -> 11.6 us  [per_device(): lax.all_to_all(send_cot, 'head', split_axis=0, concat_axis=0, tiled=True)]
    all_to_all x1 -> x0, starting transfers between devices: 4.26 us -> none  [per_device(): lax.all_to_all(send_query, 'head', split_axis=0, concat_axis=0, tiled=True)]
    all_to_all x1, waiting for transfers between devices: 2.51 us -> 0.01 us  [per_device(): lax.all_to_all(filled, 'head', split_axis=0, concat_axis=0, tiled=True)]
    unnamed x63 -> x86, local copies, waits for them, and re-layouts: 3.07 us -> 5.3 us
  transfers between devices with their start and end apart: 9 -> 23, of which waited for: 8 -> 15; matrix products, arithmetic and copies ran while one was open for 24% -> 20% of each run, Pallas kernels for 0% -> 0%
where the time goes in v1:
time: 251 us; the launch traced here: 250 us
  starting transfers between devices  78.4 us (31%)
  waiting for transfers between devices  76.2 us (30%)
  local copies, waits for them, and re-layouts  46 us (18%)
  other arithmetic  23 us (9%)
  matrix products  17.2 us (7%)
  blocking collectives  5.42 us (2%)
  between operations  3.93 us (2%)
    ppermute x15, starting transfers between devices, exchange_directly(): lax.ppermute(sent, axis, [(d, (d + far) % ways) for d in range(ways)])  40.5 us
    ppermute x15, waiting for transfers between devices, exchange_directly(): lax.ppermute(sent, axis, [(d, (d + far) % ways) for d in range(ways)])  23.4 us
    gather x4, local copies, waits for them, and re-layouts, collect(): buffer.reshape(buffer_rows, buffer.shape[-1])[target]  16.1 us
    all_to_all x1, waiting for transfers between devices, per_device(): lax.all_to_all(jnp.stack(kgrad_list, axis=1), 'head', split_axis=0, conca...  13.4 us
    all_to_all x1, waiting for transfers between devices, per_device(): lax.all_to_all(send_cot, 'head', split_axis=0, concat_axis=0, tiled=True)  11.6 us
    scatter x3, local copies, waits for them, and re-layouts, spread_out(): jnp.zeros((buffer_rows, flat_rows.shape[-1]), flat_rows.dtype).at[target]  11.3 us
    all_to_all x1, waiting for transfers between devices, per_device(): lax.all_to_all(send_value, 'head', split_axis=0, concat_axis=0, tiled=True)  11.1 us
    all_to_all x1, waiting for transfers between devices, per_device(): lax.all_to_all(jnp.stack(out_list, axis=1), 'head', split_axis=0, concat_...  8.63 us
  transfers between devices with their start and end apart: 23, of which 15 were waited for; matrix products, arithmetic and copies ran while one was open for 20% of the time, Pallas kernels for 0%

profile of v1, /device:TPU:0, one launch (start us, length us, event | category | flops | bytes accessed | tf_op | source)
XLA Modules:
  0.0 250.2 jit_solution(5730179948185459177)
XLA Ops:
  2.3 7.6 %scatter_custom_fusion = bf16[2048]{0:T(1024)(128)(2,1)S(1)} fusion(s32[1024]{0:T(1024)S(1)} %bitcast.237, bf16[1024]{0:T(1024)(128)(2,1)S(1)} %broadcast.377, bf16[]{:T(256)} %constant.423.clone.1), kind=kCustom, calls=%fused_computation.152 | custom fusion | bytes 4098 | tf_op jit(solution)/shard_map/scatter | solution.py:220
  10.6 7.4 %all-to-all-start = ((bf16[16,4,32]{2,1,0:T(4,128)(2,1)}), bf16[16,4,32]{2,1,0:T(4,128)(2,1)S(1)}, u32[]{:S(2)}, u32[]{:S(2)}) async-start(bf16[16,4,32]{2,1,0:T(4,128)(2,1)} %reshape.293), calls=%async_computation | async-start | bytes 32768 | tf_op jit(solution)/shard_map/all_to_all | solution.py:228
  18.0 3.3 %scatter_custom_fusion.1 = bf16[2048,128]{1,0:T(8,128)(2,1)S(1)} fusion(s32[1024]{0:T(1024)S(1)} %bitcast.238, bf16[1,128,8,128]{3,2,1,0:T(8,128)(2,1)S(1)} %copy-done, bf16[]{:T(256)} %constant.423.clone.1), kind=kCustom, calls=%fused_computation.99 | custom fusion | bytes 786434 | tf_op jit(solution)/shard_map/scatter | solution.py:202
  22.1 1.6 collective-permute-start.13
  23.7 2.3 collective-permute-start.12
  25.9 1.5 collective-permute-start.11
  27.4 1.9 collective-permute-start
  31.3 4.0 %scatter_custom_fusion.3 = bf16[2048,128]{1,0:T(8,128)(2,1)} fusion(s32[1024]{0:T(1024)S(1)} %bitcast.239, bf16[1,128,8,128]{3,2,1,0:T(8,128)(2,1)S(1)} %copy-done.20, bf16[]{:T(256)} %constant.423.clone.1), kind=kCustom, calls=%fused_computation.95 | custom fusion | bytes 786434 | tf_op jit(solution)/shard_map/scatter | solution.py:202
  35.3 4.0 %scatter_custom_fusion.2 = bf16[2048,128]{1,0:T(8,128)(2,1)} fusion(s32[1024]{0:T(1024)S(1)} %bitcast.240, bf16[1,128,8,128]{3,2,1,0:T(8,128)(2,1)S(1)} %copy-done.21, bf16[]{:T(256)} %constant.423.clone.1), kind=kCustom, calls=%fused_computation.97 | custom fusion | bytes 786434 | tf_op jit(solution)/shard_map/scatter | solution.py:202
  39.3 4.5 %scatter_custom_fusion.4 = bf16[2048,128]{1,0:T(8,128)(2,1)} fusion(s32[1024]{0:T(1024)S(1)} %bitcast.241, bf16[1,128,8,128]{3,2,1,0:T(8,128)(2,1)S(1)} %copy-done.4, f32[1024]{0:T(1024)S(1)} %exponential_divide_fusion, bf16[]{:T(256)} %constant.423.clone.1), kind=kCustom, calls=%fused_computation.94 | custom fusion | flops 393216 | bytes 790530 | tf_op jit(solution)/shard_map/scatter | solution.py:202
  43.8 3.6 %all-to-all-start.1 = ((bf16[16,4,32,128]{3,2,1,0:T(8,128)(2,1)}), bf16[16,4,32,128]{3,2,1,0:T(8,128)(2,1)S(1)}, u32[]{:S(2)}, u32[]{:S(2)}) async-start(bf16[16,4,32,128]{3,2,1,0:T(8,128)(2,1)} %bitcast.7), calls=%async_computation.1 | async-start | bytes 1048576 | tf_op jit(solution)/shard_map/all_to_all | solution.py:226
  47.8 4.6 %collective-permute-start.1 = (bf16[1,4,32,128]{3,2,1,0:T(8,128)(2,1)S(1)}, bf16[1,4,32,128]{3,2,1,0:T(8,128)(2,1)S(1)}, u32[]{:S(2)}, u32[]{:S(2)}) collective-permute-start(bf16[1,4,32,128]{3,2,1,0:T(8,128)(2,1)S(1)} %get-tuple-element.1338), channel_id=1, source_target_pairs={{0,14},{1,15},{2,0},{3,1},{4,2},{5,3},{6,4},{7,5},{8,6},{9,7},{10,... | collective-permute-start | bytes 98312 | tf_op jit(solution)/shard_map/ppermute | solution.py:20
  52.4 5.0 %collective-permute-done.1 = bf16[1,4,32,128]{3,2,1,0:T(8,128)(2,1)S(1)} collective-permute-done((bf16[1,4,32,128]{3,2,1,0:T(8,128)(2,1)S(1)}, bf16[1,4,32,128]{3,2,1,0:T(8,128)(2,1)S(1)}, u32[]{:S(2)}, u32[]{:S(2)}) %collective-permute-start.1) | collective-permute-done | bytes 32800 | tf_op jit(solution)/shard_map/ppermute | solution.py:20
  57.5 2.6 %collective-permute-start.2 = (bf16[1,4,32,128]{3,2,1,0:T(8,128)(2,1)S(1)}, bf16[1,4,32,128]{3,2,1,0:T(8,128)(2,1)S(1)}, u32[]{:S(2)}, u32[]{:S(2)}) collective-permute-start(bf16[1,4,32,128]{3,2,1,0:T(8,128)(2,1)S(1)} %get-tuple-element.1337), channel_id=1, source_target_pairs={{0,13},{1,14},{2,15},{3,0},{4,1},{5,2},{6,3},{7,4},{8,5},{9,6},{10... | collective-permute-start | bytes 98312 | tf_op jit(solution)/shard_map/ppermute | solution.py:20
  60.1 1.6 collective-permute-done.2
  61.7 3.3 %collective-permute-start.3 = (bf16[1,4,32,128]{3,2,1,0:T(8,128)(2,1)S(1)}, bf16[1,4,32,128]{3,2,1,0:T(8,128)(2,1)S(1)}, u32[]{:S(2)}, u32[]{:S(2)}) collective-permute-start(bf16[1,4,32,128]{3,2,1,0:T(8,128)(2,1)S(1)} %get-tuple-element.1336), channel_id=1, source_target_pairs={{0,12},{1,13},{2,14},{3,15},{4,0},{5,1},{6,2},{7,3},{8,4},{9,5},{1... | collective-permute-start | bytes 98312 | tf_op jit(solution)/shard_map/ppermute | solution.py:20
  65.0 2.6 %collective-permute-done.3 = bf16[1,4,32,128]{3,2,1,0:T(8,128)(2,1)S(1)} collective-permute-done((bf16[1,4,32,128]{3,2,1,0:T(8,128)(2,1)S(1)}, bf16[1,4,32,128]{3,2,1,0:T(8,128)(2,1)S(1)}, u32[]{:S(2)}, u32[]{:S(2)}) %collective-permute-start.3) | collective-permute-done | bytes 32800 | tf_op jit(solution)/shard_map/ppermute | solution.py:20
  67.6 1.5 collective-permute-start.4
  69.1 1.8 collective-permute-done.4
  70.9 4.4 %collective-permute-start.5 = (bf16[1,4,32,128]{3,2,1,0:T(8,128)(2,1)S(1)}, bf16[1,4,32,128]{3,2,1,0:T(8,128)(2,1)S(1)}, u32[]{:S(2)}, u32[]{:S(2)}) collective-permute-start(bf16[1,4,32,128]{3,2,1,0:T(8,128)(2,1)S(1)} %get-tuple-element.1334), channel_id=1, source_target_pairs={{0,10},{1,11},{2,12},{3,13},{4,14},{5,15},{6,0},{7,1},{8,2},{9,3},... | collective-permute-start | bytes 98312 | tf_op jit(solution)/shard_map/ppermute | solution.py:20
  75.3 2.8 %collective-permute-done.5 = bf16[1,4,32,128]{3,2,1,0:T(8,128)(2,1)S(1)} collective-permute-done((bf16[1,4,32,128]{3,2,1,0:T(8,128)(2,1)S(1)}, bf16[1,4,32,128]{3,2,1,0:T(8,128)(2,1)S(1)}, u32[]{:S(2)}, u32[]{:S(2)}) %collective-permute-start.5) | collective-permute-done | bytes 32800 | tf_op jit(solution)/shard_map/ppermute | solution.py:20
  78.1 1.9 collective-permute-start.6
  80.0 2.3 collective-permute-done.6
  82.3 4.0 %collective-permute-start.7 = (bf16[1,4,32,128]{3,2,1,0:T(8,128)(2,1)S(1)}, bf16[1,4,32,128]{3,2,1,0:T(8,128)(2,1)S(1)}, u32[]{:S(2)}, u32[]{:S(2)}) collective-permute-start(bf16[1,4,32,128]{3,2,1,0:T(8,128)(2,1)S(1)} %get-tuple-element.1332), channel_id=1, source_target_pairs={{0,8},{1,9},{2,10},{3,11},{4,12},{5,13},{6,14},{7,15},{8,0},{9,1},... | collective-permute-start | bytes 98312 | tf_op jit(solution)/shard_map/ppermute | solution.py:20
  86.3 1.9 collective-permute-done.7
  88.2 2.7 %collective-permute-start.8 = (bf16[1,4,32,128]{3,2,1,0:T(8,128)(2,1)S(1)}, bf16[1,4,32,128]{3,2,1,0:T(8,128)(2,1)S(1)}, u32[]{:S(2)}, u32[]{:S(2)}) collective-permute-start(bf16[1,4,32,128]{3,2,1,0:T(8,128)(2,1)S(1)} %get-tuple-element.1331), channel_id=1, source_target_pairs={{0,7},{1,8},{2,9},{3,10},{4,11},{5,12},{6,13},{7,14},{8,15},{9,0},... | collective-permute-start | bytes 98312 | tf_op jit(solution)/shard_map/ppermute | solution.py:20
  90.9 1.6 collective-permute-done.8
  92.5 4.9 %collective-permute-start.9 = (bf16[1,4,32,128]{3,2,1,0:T(8,128)(2,1)S(1)}, bf16[1,4,32,128]{3,2,1,0:T(8,128)(2,1)S(1)}, u32[]{:S(2)}, u32[]{:S(2)}) collective-permute-start(bf16[1,4,32,128]{3,2,1,0:T(8,128)(2,1)S(1)} %get-tuple-element.1330), channel_id=1, source_target_pairs={{0,6},{1,7},{2,8},{3,9},{4,10},{5,11},{6,12},{7,13},{8,14},{9,15},... | collective-permute-start | bytes 98312 | tf_op jit(solution)/shard_map/ppermute | solution.py:20
  97.3 1.6 collective-permute-done.9
  98.9 3.0 %collective-permute-start.10 = (bf16[1,4,32,128]{3,2,1,0:T(8,128)(2,1)S(1)}, bf16[1,4,32,128]{3,2,1,0:T(8,128)(2,1)S(1)}, u32[]{:S(2)}, u32[]{:S(2)}) collective-permute-start(bf16[1,4,32,128]{3,2,1,0:T(8,128)(2,1)S(1)} %get-tuple-element.1329), channel_id=1, source_target_pairs={{0,5},{1,6},{2,7},{3,8},{4,9},{5,10},{6,11},{7,12},{8,13},{9,14},{... | collective-permute-start | bytes 98312 | tf_op jit(solution)/shard_map/ppermute | solution.py:20
  101.9 2.1 collective-permute-done.10
  104.2 6.2 %all-to-all-start.4 = ((bf16[16,4,32,128]{3,2,1,0:T(8,128)(2,1)}), bf16[16,4,32,128]{3,2,1,0:T(8,128)(2,1)S(1)}, u32[]{:S(2)}, u32[]{:S(2)}) async-start(bf16[16,4,32,128]{3,2,1,0:T(8,128)(2,1)} %bitcast.36), calls=%async_computation.4 | async-start | bytes 1048576 | tf_op jit(solution)/shard_map/all_to_all | solution.py:259
  113.0 11.6 %all-to-all-done.4 = bf16[16,4,32,128]{3,2,1,0:T(8,128)(2,1)S(1)} async-done(((bf16[16,4,32,128]{3,2,1,0:T(8,128)(2,1)}), bf16[16,4,32,128]{3,2,1,0:T(8,128)(2,1)S(1)}, u32[]{:S(2)}, u32[]{:S(2)}) %all-to-all-start.4) | async-done | bytes 524320 | tf_op jit(solution)/shard_map/all_to_all | solution.py:259
  124.6 4.2 %all-to-all-start.2 = ((bf16[16,4,32,128]{3,2,1,0:T(8,128)(2,1)}), bf16[16,4,32,128]{3,2,1,0:T(8,128)(2,1)S(1)}, u32[]{:S(2)}, u32[]{:S(2)}) async-start(bf16[16,4,32,128]{3,2,1,0:T(8,128)(2,1)} %bitcast.11), calls=%async_computation.2 | async-start | bytes 1048576 | tf_op jit(solution)/shard_map/all_to_all | solution.py:227
  131.0 1.0 convolution_convert_fusion.1
  132.0 11.1 %all-to-all-done.2 = bf16[16,4,32,128]{3,2,1,0:T(8,128)(2,1)S(1)} async-done(((bf16[16,4,32,128]{3,2,1,0:T(8,128)(2,1)}), bf16[16,4,32,128]{3,2,1,0:T(8,128)(2,1)S(1)}, u32[]{:S(2)}, u32[]{:S(2)}) %all-to-all-start.2) | async-done | bytes 524320 | tf_op jit(solution)/shard_map/all_to_all | solution.py:227
  143.8 1.1 multiply_reduce_fusion.1
  145.8 1.0 fusion.14
  149.0 1.1 multiply_reduce_fusion.3
  150.2 1.3 fusion.7
  151.4 1.0 fusion.12
  154.7 1.1 multiply_reduce_fusion.2
  159.7 0.9 pad_maximum_fusion.3
  160.6 4.2 %all-to-all-start.7 = ((bf16[16,4,32,128]{3,2,1,0:T(8,128)(2,1)}), bf16[16,4,32,128]{3,2,1,0:T(8,128)(2,1)S(1)}, u32[]{:S(2)}, u32[]{:S(2)}) async-start(bf16[16,4,32,128]{3,2,1,0:T(8,128)(2,1)} %pad_maximum_fusion.3), calls=%async_computation.7 | async-start | bytes 1048576 | tf_op jit(solution)/shard_map/all_to_all | solution.py:286
  164.8 1.2 fusion.13
  166.1 1.1 multiply_reduce_fusion
  167.2 1.6 fusion.4
  170.9 8.2 %all-to-all-done.7 = bf16[16,4,32,128]{3,2,1,0:T(8,128)(2,1)S(1)} async-done(((bf16[16,4,32,128]{3,2,1,0:T(8,128)(2,1)}), bf16[16,4,32,128]{3,2,1,0:T(8,128)(2,1)S(1)}, u32[]{:S(2)}, u32[]{:S(2)}) %all-to-all-start.7) | async-done | bytes 524320 | tf_op jit(solution)/shard_map/all_to_all | solution.py:286
  179.1 4.2 %all-to-all-start.6 = ((bf16[16,4,32,128]{3,2,1,0:T(8,128)(2,1)}), bf16[16,4,32,128]{3,2,1,0:T(8,128)(2,1)S(1)}, u32[]{:S(2)}, u32[]{:S(2)}) async-start(bf16[16,4,32,128]{3,2,1,0:T(8,128)(2,1)} %pad_maximum_fusion.2), calls=%async_computation.6 | async-start | bytes 1048576 | tf_op jit(solution)/shard_map/all_to_all | solution.py:283
  184.2 13.4 %all-to-all-done.6 = bf16[16,4,32,128]{3,2,1,0:T(8,128)(2,1)S(1)} async-done(((bf16[16,4,32,128]{3,2,1,0:T(8,128)(2,1)}), bf16[16,4,32,128]{3,2,1,0:T(8,128)(2,1)S(1)}, u32[]{:S(2)}, u32[]{:S(2)}) %all-to-all-start.6) | async-done | bytes 524320 | tf_op jit(solution)/shard_map/all_to_all | solution.py:283
  197.5 4.2 %all-to-all-start.3 = ((bf16[16,4,32,128]{3,2,1,0:T(8,128)(2,1)}), bf16[16,4,32,128]{3,2,1,0:T(8,128)(2,1)S(1)}, u32[]{:S(2)}, u32[]{:S(2)}) async-start(bf16[16,4,32,128]{3,2,1,0:T(8,128)(2,1)} %pad_maximum_fusion), calls=%async_computation.3 | async-start | bytes 1048576 | tf_op jit(solution)/shard_map/all_to_all | solution.py:256
  201.7 1.3 fusion.10
  203.0 1.2 multiply_reduce_fusion.6
  207.3 8.6 %all-to-all-done.3 = bf16[16,4,32,128]{3,2,1,0:T(8,128)(2,1)S(1)} async-done(((bf16[16,4,32,128]{3,2,1,0:T(8,128)(2,1)}), bf16[16,4,32,128]{3,2,1,0:T(8,128)(2,1)S(1)}, u32[]{:S(2)}, u32[]{:S(2)}) %all-to-all-start.3) | async-done | bytes 524320 | tf_op jit(solution)/shard_map/all_to_all | solution.py:256
  216.0 4.2 %all-to-all-start.5 = ((bf16[16,4,32,128]{3,2,1,0:T(8,128)(2,1)}), bf16[16,4,32,128]{3,2,1,0:T(8,128)(2,1)S(1)}, u32[]{:S(2)}, u32[]{:S(2)}) async-start(bf16[16,4,32,128]{3,2,1,0:T(8,128)(2,1)} %pad_maximum_fusion.1), calls=%async_computation.5 | async-start | bytes 1048576 | tf_op jit(solution)/shard_map/all_to_all | solution.py:280
  220.1 1.3 multiply_reduce_fusion.8
  222.7 1.3 multiply_reduce_fusion.7
  224.6 1.3 multiply_reduce_fusion.5
  226.6 5.4 %psum.7 = f32[4]{0:T(128)} all-reduce(f32[4]{0:T(128)S(1)} %pad_maximum_fusion.4), channel_id=1, replica_groups=mesh['dp'=2,'head'=16] {'dp'}, use_global_device_ids=true, to_apply=%region_28.30 | all-reduce | flops 4 | bytes 32 | tf_op jit(solution)/shard_map/psum | solution.py:290
  232.0 4.3 %gather_fusion.3 = bf16[1024,128]{1,0:T(8,128)(2,1)} fusion(bf16[2048,128]{1,0:T(8,128)(2,1)S(1)} %bitcast.179, s32[1024]{0:T(1024)S(1)} %broadcast_clamp_fusion), kind=kCustom, calls=%fused_computation.3 | custom fusion | bytes 528384 | tf_op jit(solution)/shard_map/gather | solution.py:207
  236.3 4.3 %gather_fusion.2 = bf16[1024,128]{1,0:T(8,128)(2,1)} fusion(bf16[2048,128]{1,0:T(8,128)(2,1)S(1)} %bitcast.180, s32[1024]{0:T(1024)S(1)} %broadcast_clamp_fusion), kind=kCustom, calls=%fused_computation.2 | custom fusion | bytes 528384 | tf_op jit(solution)/shard_map/gather | solution.py:207
  240.6 3.2 %gather_fusion = bf16[1024,128]{1,0:T(8,128)(2,1)S(1)} fusion(bf16[2048,128]{1,0:T(8,128)(2,1)S(1)} %bitcast.181, s32[1024]{0:T(1024)S(1)} %broadcast_clamp_fusion), kind=kCustom, calls=%fused_computation | custom fusion | bytes 528384 | tf_op jit(solution)/shard_map/gather | solution.py:207
  244.3 4.3 %gather_fusion.1 = bf16[1024,128]{1,0:T(8,128)(2,1)} fusion(bf16[2048,128]{1,0:T(8,128)(2,1)S(1)} %bitcast.182, s32[1024]{0:T(1024)S(1)} %broadcast_clamp_fusion), kind=kCustom, calls=%fused_computation.1 | custom fusion | bytes 528384 | tf_op jit(solution)/shard_map/gather | solution.py:207
  248.6 0.9 fusion.25
  (165 shorter events, 27.7 us)
Async XLA Ops:
  0.6 17.4 %copy-start = (bf16[1,128,8,128]{3,2,1,0:T(8,128)(2,1)S(1)}, bf16[1,128,8,128]{3,2,1,0:T(8,128)(2,1)}, u32[]{:S(2)}) copy-start(bf16[1,128,8,128]{3,2,1,0:T(8,128)(2,1)} %param.10) | copy-start | bytes 786436
  0.6 0.8 copy-start.33
  10.6 33.2 %all-to-all-start = ((bf16[16,4,32]{2,1,0:T(4,128)(2,1)}), bf16[16,4,32]{2,1,0:T(4,128)(2,1)S(1)}, u32[]{:S(2)}, u32[]{:S(2)}) async-start(bf16[16,4,32]{2,1,0:T(4,128)(2,1)} %reshape.293), calls=%async_computation | async-start | bytes 32768 | tf_op jit(solution)/shard_map/all_to_all | solution.py:228
  21.6 7.7 %copy-start.32 = (f32[1,128,8]{1,2,0:T(8,128)S(1)}, f32[1,128,8]{1,2,0:T(8,128)}, u32[]{:S(2)}) copy-start(f32[1,128,8]{1,2,0:T(8,128)} %param.13) | copy-start | bytes 12292
  21.6 82.5 %collective-permute-start.14 = (bf16[1,4,32,128]{3,2,1,0:T(8,128)(2,1)S(1)}, bf16[1,4,32,128]{3,2,1,0:T(8,128)(2,1)S(1)}, u32[]{:S(2)}, u32[]{:S(2)}) collective-permute-start(bf16[1,4,32,128]{3,2,1,0:T(8,128)(2,1)S(1)} %get-tuple-element.1325), channel_id=1, source_target_pairs={{0,1},{1,2},{2,3},{3,4},{4,5},{5,6},{6,7},{7,8},{8,9},{9,10},{10,1... | collective-permute-start | bytes 98312 | tf_op jit(solution)/shard_map/ppermute | solution.py:20
  22.1 82.1 %collective-permute-start.13 = (bf16[1,4,32,128]{3,2,1,0:T(8,128)(2,1)S(1)}, bf16[1,4,32,128]{3,2,1,0:T(8,128)(2,1)S(1)}, u32[]{:S(2)}, u32[]{:S(2)}) collective-permute-start(bf16[1,4,32,128]{3,2,1,0:T(8,128)(2,1)S(1)} %get-tuple-element.1326), channel_id=1, source_target_pairs={{0,2},{1,3},{2,4},{3,5},{4,6},{5,7},{6,8},{7,9},{8,10},{9,11},{10,... | collective-permute-start | bytes 98312 | tf_op jit(solution)/shard_map/ppermute | solution.py:20
  23.7 80.4 %collective-permute-start.12 = (bf16[1,4,32,128]{3,2,1,0:T(8,128)(2,1)S(1)}, bf16[1,4,32,128]{3,2,1,0:T(8,128)(2,1)S(1)}, u32[]{:S(2)}, u32[]{:S(2)}) collective-permute-start(bf16[1,4,32,128]{3,2,1,0:T(8,128)(2,1)S(1)} %get-tuple-element.1327), channel_id=1, source_target_pairs={{0,3},{1,4},{2,5},{3,6},{4,7},{5,8},{6,9},{7,10},{8,11},{9,12},{10... | collective-permute-start | bytes 98312 | tf_op jit(solution)/shard_map/ppermute | solution.py:20
  25.9 78.1 %collective-permute-start.11 = (bf16[1,4,32,128]{3,2,1,0:T(8,128)(2,1)S(1)}, bf16[1,4,32,128]{3,2,1,0:T(8,128)(2,1)S(1)}, u32[]{:S(2)}, u32[]{:S(2)}) collective-permute-start(bf16[1,4,32,128]{3,2,1,0:T(8,128)(2,1)S(1)} %get-tuple-element.1328), channel_id=1, source_target_pairs={{0,4},{1,5},{2,6},{3,7},{4,8},{5,9},{6,10},{7,11},{8,12},{9,13},{1... | collective-permute-start | bytes 98312 | tf_op jit(solution)/shard_map/ppermute | solution.py:20
  27.4 3.9 %copy-start.20 = (bf16[1,128,8,128]{3,2,1,0:T(8,128)(2,1)S(1)}, bf16[1,128,8,128]{3,2,1,0:T(8,128)(2,1)}, u32[]{:S(2)}) copy-start(bf16[1,128,8,128]{3,2,1,0:T(8,128)(2,1)} %param.12) | copy-start | bytes 786436
  27.4 20.4 %collective-permute-start = (bf16[1,4,32,128]{3,2,1,0:T(8,128)(2,1)S(1)}, bf16[1,4,32,128]{3,2,1,0:T(8,128)(2,1)S(1)}, u32[]{:S(2)}, u32[]{:S(2)}) collective-permute-start(bf16[1,4,32,128]{3,2,1,0:T(8,128)(2,1)S(1)} %get-tuple-element.1339), channel_id=1, source_target_pairs={{0,15},{1,0},{2,1},{3,2},{4,3},{5,4},{6,5},{7,6},{8,7},{9,8},{10,9... | collective-permute-start | bytes 98312 | tf_op jit(solution)/shard_map/ppermute | solution.py:20
  30.0 0.7 copy-start.34
  31.3 4.0 %copy-start.21 = (bf16[1,128,8,128]{3,2,1,0:T(8,128)(2,1)S(1)}, bf16[1,128,8,128]{3,2,1,0:T(8,128)(2,1)}, u32[]{:S(2)}) copy-start(bf16[1,128,8,128]{3,2,1,0:T(8,128)(2,1)} %param.11) | copy-start | bytes 786436
  35.3 4.0 %copy-start.4 = (bf16[1,128,8,128]{3,2,1,0:T(8,128)(2,1)S(1)}, bf16[1,128,8,128]{3,2,1,0:T(8,128)(2,1)}, u32[]{:S(2)}) copy-start(bf16[1,128,8,128]{3,2,1,0:T(8,128)(2,1)} %param.15) | copy-start | bytes 786436
  43.8 60.4 %all-to-all-start.1 = ((bf16[16,4,32,128]{3,2,1,0:T(8,128)(2,1)}), bf16[16,4,32,128]{3,2,1,0:T(8,128)(2,1)S(1)}, u32[]{:S(2)}, u32[]{:S(2)}) async-start(bf16[16,4,32,128]{3,2,1,0:T(8,128)(2,1)} %bitcast.7), calls=%async_computation.1 | async-start | bytes 1048576 | tf_op jit(solution)/shard_map/all_to_all | solution.py:226
  47.8 9.6 %collective-permute-start.1 = (bf16[1,4,32,128]{3,2,1,0:T(8,128)(2,1)S(1)}, bf16[1,4,32,128]{3,2,1,0:T(8,128)(2,1)S(1)}, u32[]{:S(2)}, u32[]{:S(2)}) collective-permute-start(bf16[1,4,32,128]{3,2,1,0:T(8,128)(2,1)S(1)} %get-tuple-element.1338), channel_id=1, source_target_pairs={{0,14},{1,15},{2,0},{3,1},{4,2},{5,3},{6,4},{7,5},{8,6},{9,7},{10,... | collective-permute-start | bytes 98312 | tf_op jit(solution)/shard_map/ppermute | solution.py:20
  57.5 4.2 %collective-permute-start.2 = (bf16[1,4,32,128]{3,2,1,0:T(8,128)(2,1)S(1)}, bf16[1,4,32,128]{3,2,1,0:T(8,128)(2,1)S(1)}, u32[]{:S(2)}, u32[]{:S(2)}) collective-permute-start(bf16[1,4,32,128]{3,2,1,0:T(8,128)(2,1)S(1)} %get-tuple-element.1337), channel_id=1, source_target_pairs={{0,13},{1,14},{2,15},{3,0},{4,1},{5,2},{6,3},{7,4},{8,5},{9,6},{10... | collective-permute-start | bytes 98312 | tf_op jit(solution)/shard_map/ppermute | solution.py:20
  61.7 5.9 %collective-permute-start.3 = (bf16[1,4,32,128]{3,2,1,0:T(8,128)(2,1)S(1)}, bf16[1,4,32,128]{3,2,1,0:T(8,128)(2,1)S(1)}, u32[]{:S(2)}, u32[]{:S(2)}) collective-permute-start(bf16[1,4,32,128]{3,2,1,0:T(8,128)(2,1)S(1)} %get-tuple-element.1336), channel_id=1, source_target_pairs={{0,12},{1,13},{2,14},{3,15},{4,0},{5,1},{6,2},{7,3},{8,4},{9,5},{1... | collective-permute-start | bytes 98312 | tf_op jit(solution)/shard_map/ppermute | solution.py:20
  67.6 3.3 %collective-permute-start.4 = (bf16[1,4,32,128]{3,2,1,0:T(8,128)(2,1)S(1)}, bf16[1,4,32,128]{3,2,1,0:T(8,128)(2,1)S(1)}, u32[]{:S(2)}, u32[]{:S(2)}) collective-permute-start(bf16[1,4,32,128]{3,2,1,0:T(8,128)(2,1)S(1)} %get-tuple-element.1335), channel_id=1, source_target_pairs={{0,11},{1,12},{2,13},{3,14},{4,15},{5,0},{6,1},{7,2},{8,3},{9,4},{... | collective-permute-start | bytes 98312 | tf_op jit(solution)/shard_map/ppermute | solution.py:20
  70.9 7.2 %collective-permute-start.5 = (bf16[1,4,32,128]{3,2,1,0:T(8,128)(2,1)S(1)}, bf16[1,4,32,128]{3,2,1,0:T(8,128)(2,1)S(1)}, u32[]{:S(2)}, u32[]{:S(2)}) collective-permute-start(bf16[1,4,32,128]{3,2,1,0:T(8,128)(2,1)S(1)} %get-tuple-element.1334), channel_id=1, source_target_pairs={{0,10},{1,11},{2,12},{3,13},{4,14},{5,15},{6,0},{7,1},{8,2},{9,3},... | collective-permute-start | bytes 98312 | tf_op jit(solution)/shard_map/ppermute | solution.py:20
  78.1 4.2 %collective-permute-start.6 = (bf16[1,4,32,128]{3,2,1,0:T(8,128)(2,1)S(1)}, bf16[1,4,32,128]{3,2,1,0:T(8,128)(2,1)S(1)}, u32[]{:S(2)}, u32[]{:S(2)}) collective-permute-start(bf16[1,4,32,128]{3,2,1,0:T(8,128)(2,1)S(1)} %get-tuple-element.1333), channel_id=1, source_target_pairs={{0,9},{1,10},{2,11},{3,12},{4,13},{5,14},{6,15},{7,0},{8,1},{9,2},... | collective-permute-start | bytes 98312 | tf_op jit(solution)/shard_map/ppermute | solution.py:20
  82.3 5.8 %collective-permute-start.7 = (bf16[1,4,32,128]{3,2,1,0:T(8,128)(2,1)S(1)}, bf16[1,4,32,128]{3,2,1,0:T(8,128)(2,1)S(1)}, u32[]{:S(2)}, u32[]{:S(2)}) collective-permute-start(bf16[1,4,32,128]{3,2,1,0:T(8,128)(2,1)S(1)} %get-tuple-element.1332), channel_id=1, source_target_pairs={{0,8},{1,9},{2,10},{3,11},{4,12},{5,13},{6,14},{7,15},{8,0},{9,1},... | collective-permute-start | bytes 98312 | tf_op jit(solution)/shard_map/ppermute | solution.py:20
  88.2 4.3 %collective-permute-start.8 = (bf16[1,4,32,128]{3,2,1,0:T(8,128)(2,1)S(1)}, bf16[1,4,32,128]{3,2,1,0:T(8,128)(2,1)S(1)}, u32[]{:S(2)}, u32[]{:S(2)}) collective-permute-start(bf16[1,4,32,128]{3,2,1,0:T(8,128)(2,1)S(1)} %get-tuple-element.1331), channel_id=1, source_target_pairs={{0,7},{1,8},{2,9},{3,10},{4,11},{5,12},{6,13},{7,14},{8,15},{9,0},... | collective-permute-start | bytes 98312 | tf_op jit(solution)/shard_map/ppermute | solution.py:20
  92.5 6.5 %collective-permute-start.9 = (bf16[1,4,32,128]{3,2,1,0:T(8,128)(2,1)S(1)}, bf16[1,4,32,128]{3,2,1,0:T(8,128)(2,1)S(1)}, u32[]{:S(2)}, u32[]{:S(2)}) collective-permute-start(bf16[1,4,32,128]{3,2,1,0:T(8,128)(2,1)S(1)} %get-tuple-element.1330), channel_id=1, source_target_pairs={{0,6},{1,7},{2,8},{3,9},{4,10},{5,11},{6,12},{7,13},{8,14},{9,15},... | collective-permute-start | bytes 98312 | tf_op jit(solution)/shard_map/ppermute | solution.py:20
  98.9 5.1 %collective-permute-start.10 = (bf16[1,4,32,128]{3,2,1,0:T(8,128)(2,1)S(1)}, bf16[1,4,32,128]{3,2,1,0:T(8,128)(2,1)S(1)}, u32[]{:S(2)}, u32[]{:S(2)}) collective-permute-start(bf16[1,4,32,128]{3,2,1,0:T(8,128)(2,1)S(1)} %get-tuple-element.1329), channel_id=1, source_target_pairs={{0,5},{1,6},{2,7},{3,8},{4,9},{5,10},{6,11},{7,12},{8,13},{9,14},{... | collective-permute-start | bytes 98312 | tf_op jit(solution)/shard_map/ppermute | solution.py:20
  104.2 20.4 %all-to-all-start.4 = ((bf16[16,4,32,128]{3,2,1,0:T(8,128)(2,1)}), bf16[16,4,32,128]{3,2,1,0:T(8,128)(2,1)S(1)}, u32[]{:S(2)}, u32[]{:S(2)}) async-start(bf16[16,4,32,128]{3,2,1,0:T(8,128)(2,1)} %bitcast.36), calls=%async_computation.4 | async-start | bytes 1048576 | tf_op jit(solution)/shard_map/all_to_all | solution.py:259
  111.3 0.8 copy-start.18
  111.3 41.1 %copy-start.15 = (bf16[16,1,32,128]{3,2,1,0:T(8,128)(2,1)}, bf16[16,1,32,128]{3,2,1,0:T(8,128)(2,1)S(1)}, u32[]{:S(2)}) copy-start(bf16[16,1,32,128]{3,2,1,0:T(8,128)(2,1)S(1)} %get-tuple-element.1319) | copy-start | bytes 393220
  112.0 0.7 copy-start.12
  112.0 34.7 %copy-start.10 = (bf16[16,1,32,128]{3,2,1,0:T(8,128)(2,1)}, bf16[16,1,32,128]{3,2,1,0:T(8,128)(2,1)S(1)}, u32[]{:S(2)}) copy-start(bf16[16,1,32,128]{3,2,1,0:T(8,128)(2,1)S(1)} %get-tuple-element.1313) | copy-start | bytes 393220
  112.0 40.4 %copy-start.8 = (bf16[16,1,32,128]{3,2,1,0:T(8,128)(2,1)}, bf16[16,1,32,128]{3,2,1,0:T(8,128)(2,1)S(1)}, u32[]{:S(2)}) copy-start(bf16[16,1,32,128]{3,2,1,0:T(8,128)(2,1)S(1)} %get-tuple-element.1316) | copy-start | bytes 393220
  124.6 18.4 %all-to-all-start.2 = ((bf16[16,4,32,128]{3,2,1,0:T(8,128)(2,1)}), bf16[16,4,32,128]{3,2,1,0:T(8,128)(2,1)S(1)}, u32[]{:S(2)}, u32[]{:S(2)}) async-start(bf16[16,4,32,128]{3,2,1,0:T(8,128)(2,1)} %bitcast.11), calls=%async_computation.2 | async-start | bytes 1048576 | tf_op jit(solution)/shard_map/all_to_all | solution.py:227
  131.0 18.0 %copy-start.30 = (bf16[16,1,32,128]{3,2,1,0:T(8,128)(2,1)}, bf16[16,1,32,128]{3,2,1,0:T(8,128)(2,1)S(1)}, u32[]{:S(2)}) copy-start(bf16[16,1,32,128]{3,2,1,0:T(8,128)(2,1)S(1)} %get-tuple-element.1309) | copy-start | bytes 393220
  144.9 0.9 copy-start.19
  153.4 1.0 copy-start.29
  155.8 0.9 copy-start.6
  155.8 1.0 copy-start.13
  157.1 8.9 %copy-start.3 = (f32[512,512]{0,1:T(8,128)}, f32[512,512]{0,1:T(8,128)S(1)}, u32[]{:S(2)}) copy-start(f32[512,512]{0,1:T(8,128)S(1)} %get-tuple-element.1345) | copy-start | bytes 3145732
  157.8 1.0 copy-start.23
  158.8 0.9 copy-start.27
  160.6 18.4 %all-to-all-start.7 = ((bf16[16,4,32,128]{3,2,1,0:T(8,128)(2,1)}), bf16[16,4,32,128]{3,2,1,0:T(8,128)(2,1)S(1)}, u32[]{:S(2)}, u32[]{:S(2)}) async-start(bf16[16,4,32,128]{3,2,1,0:T(8,128)(2,1)} %pad_maximum_fusion.3), calls=%async_computation.7 | async-start | bytes 1048576 | tf_op jit(solution)/shard_map/all_to_all | solution.py:286
  164.8 1.3 copy-start.24
  164.8 1.3 copy-start.26
  167.2 1.6 copy-start.14
  168.8 2.0 copy-start.1
  168.8 1.0 copy-start.16
  168.9 1.1 copy-start.17
  170.9 12.4 %copy-start.22 = (bf16[512,128]{1,0:T(8,128)(2,1)S(1)}, bf16[512,128]{1,0:T(8,128)(2,1)}, u32[]{:S(2)}) copy-start(bf16[512,128]{1,0:T(8,128)(2,1)} %get-tuple-element.1355) | copy-start | bytes 393220
  170.9 12.4 %copy-start.25 = (bf16[512,128]{1,0:T(8,128)(2,1)S(1)}, bf16[512,128]{1,0:T(8,128)(2,1)}, u32[]{:S(2)}) copy-start(bf16[512,128]{1,0:T(8,128)(2,1)} %get-tuple-element.1359) | copy-start | bytes 393220
  170.9 12.4 %copy-start.28 = (bf16[512,128]{1,0:T(8,128)(2,1)S(1)}, bf16[512,128]{1,0:T(8,128)(2,1)}, u32[]{:S(2)}) copy-start(bf16[512,128]{1,0:T(8,128)(2,1)} %get-tuple-element.1357) | copy-start | bytes 393220
  170.9 12.4 %copy-start.31 = (bf16[512,128]{1,0:T(8,128)(2,1)S(1)}, bf16[512,128]{1,0:T(8,128)(2,1)}, u32[]{:S(2)}) copy-start(bf16[512,128]{1,0:T(8,128)(2,1)} %get-tuple-element.1353) | copy-start | bytes 393220
  179.1 18.4 %all-to-all-start.6 = ((bf16[16,4,32,128]{3,2,1,0:T(8,128)(2,1)}), bf16[16,4,32,128]{3,2,1,0:T(8,128)(2,1)S(1)}, u32[]{:S(2)}, u32[]{:S(2)}) async-start(bf16[16,4,32,128]{3,2,1,0:T(8,128)(2,1)} %pad_maximum_fusion.2), calls=%async_computation.6 | async-start | bytes 1048576 | tf_op jit(solution)/shard_map/all_to_all | solution.py:283
  197.5 18.4 %all-to-all-start.3 = ((bf16[16,4,32,128]{3,2,1,0:T(8,128)(2,1)}), bf16[16,4,32,128]{3,2,1,0:T(8,128)(2,1)S(1)}, u32[]{:S(2)}, u32[]{:S(2)}) async-start(bf16[16,4,32,128]{3,2,1,0:T(8,128)(2,1)} %pad_maximum_fusion), calls=%async_computation.3 | async-start | bytes 1048576 | tf_op jit(solution)/shard_map/all_to_all | solution.py:256
  201.7 2.5 copy-start.11
  204.2 0.9 copy-start.9
  205.1 1.0 copy-start.2
  205.1 1.1 copy-start.7
  216.0 28.4 %all-to-all-start.5 = ((bf16[16,4,32,128]{3,2,1,0:T(8,128)(2,1)}), bf16[16,4,32,128]{3,2,1,0:T(8,128)(2,1)S(1)}, u32[]{:S(2)}, u32[]{:S(2)}) async-start(bf16[16,4,32,128]{3,2,1,0:T(8,128)(2,1)} %pad_maximum_fusion.1), calls=%async_computation.5 | async-start | bytes 1048576 | tf_op jit(solution)/shard_map/all_to_all | solution.py:280
  240.6 3.2 %copy-start.5 = (bf16[1,128,8,128]{3,2,1,0:T(8,128)(2,1)S(1)}, bf16[1,128,8,128]{3,2,1,0:T(8,128)(2,1)}, u32[]{:S(2)}) copy-start(bf16[1,128,8,128]{3,2,1,0:T(8,128)(2,1)} %param.15) | copy-start | bytes 786436
